TPU v7x, 32 devices: a whole 2x2x4 slice. The times are simulated.
32 devices in a mesh: row: 16 (over z, y, core), col: 2 (over x).
Axes of the slice: x: 2, y: 2, z: 4, core: 2. Of those that a mesh axis runs over, the one named last changes fastest.
Arguments:
- c_matrix: bfloat16 [2, 3072, 6144], P(None, 'row', 'col'), may hold values from -6 to 6
- beta_values: bfloat16 [1, 48, 6, 128, 128], P(None, 'col'), may hold values from -0.21875 to 0.21875
- beta_rows: int32 [1, 48, 6], P(None, 'col'), may hold values from 0 to 47, as said below
- alpha_values: bfloat16 [1, 2, 16, 4, 192, 192], P(None, None, 'row'), may hold values from -0.21875 to 0.21875
- alpha_rows: int32 [1, 2, 16, 4], P(None, None, 'row'), may hold values from 0 to 31, as said below
- gaps: float32 [2, 3072, 6144], P(None, 'row', 'col'), may hold values from 0.5 to 4
Outputs:
- update: float32 [2, 3072, 6144], P(None, 'row', 'col')
Inputs may be any that keep to these rules, and one draw needn't show every extreme that they name: For every k and tile column j, beta_rows[k, j] lists 6 distinct tile rows and its first entry is j. For every k, g, r, alpha_rows[k, g, r] lists 4 distinct tile rows and its first entry is the tile column g * 16 + r.
All inputs are finite; a program needn't handle non-finite values.
Results may differ from a plain program's by a relative error of at most 0.0029.
Values may be sent and summed in bfloat16 or wider, within the bound.
A program may use at most 192 MiB of HBM per device.

v0:
```python
import jax
import jax.numpy as jnp
from jax import lax
from jax.sharding import PartitionSpec as P


def beta_products(gathered, beta_values, beta_rows):
    groups, stretch_rows, columns = gathered.shape
    local_rows = groups * stretch_rows
    tile_width = beta_values.shape[-1]
    tiled = gathered.reshape(local_rows, columns // tile_width, tile_width)
    picked = tiled[:, beta_rows]
    product = jnp.einsum(
        "rkjzt,kjzts->krjs", picked, beta_values, preferred_element_type=jnp.float32
    )
    return product.astype(jnp.bfloat16).reshape(beta_values.shape[0] * local_rows, -1)


def alpha_blocks(alpha_values, alpha_rows, row_devices, pattern):
    alpha_tiles = alpha_values[:, :, 0]
    alpha_lists = alpha_rows[:, :, 0]
    groups = alpha_lists.shape[1]
    tile_count = groups * row_devices
    onehot = (alpha_lists[..., None] == jnp.arange(tile_count, dtype=jnp.int32)).astype(
        jnp.bfloat16
    )
    onehot = onehot.reshape(onehot.shape[:3] + (groups, row_devices))
    spread = jnp.einsum(pattern, onehot, alpha_tiles, preferred_element_type=jnp.float32)
    return spread.astype(jnp.bfloat16).reshape(tile_count * alpha_tiles.shape[-1], -1)


def per_device(c_matrix, beta_values, beta_rows, alpha_values, alpha_rows, gaps):
    row_devices = lax.axis_size("row")
    groups, stretch_rows, columns = c_matrix.shape
    gathered = lax.all_gather(c_matrix, "col", axis=2, tiled=True)
    x_stack = beta_products(gathered, beta_values, beta_rows)
    spread = alpha_blocks(alpha_values, alpha_rows, row_devices, "kgzab,kgzuv->abukgv")
    strips = lax.psum_scatter(
        lax.dot_general(
            x_stack, spread, (((0,), (1,)), ((), ())), preferred_element_type=jnp.float32
        ),
        "row",
        scatter_dimension=0,
        tiled=True,
    )
    strips = strips.reshape(stretch_rows, groups, columns)
    own_part = jnp.transpose(
        lax.all_to_all(strips, "row", split_axis=2, concat_axis=0, tiled=True), (1, 2, 0)
    )
    mirrored = jnp.transpose(
        lax.all_to_all(strips, "col", split_axis=1, concat_axis=1, tiled=True), (1, 0, 2)
    )
    return (own_part + mirrored) / gaps


def solution(mesh):
    placed = (
        P(None, "row", "col"),
        P(None, "col", None, None, None),
        P(None, "col", None),
        P(None, None, "row", None, None, None),
        P(None, None, "row", None),
        P(None, "row", "col"),
    )
    return jax.shard_map(
        per_device, mesh=mesh, in_specs=placed, out_specs=P(None, "row", "col"), check_vma=False
    )
```

profile of v0, /device:TPU:15, one launch (start us, length us, event | category | flops | bytes accessed | tf_op | source)
XLA Modules:
  0.0 1066.7 jit_solution(12768925375199351323)
XLA Ops:
  6.5 0.7 all-gather.2.cloned.1.call-update
  7.3 0.7 compare_select_fusion
  8.0 0.1 copy.33
  8.1 0.1 reshape.43
  8.2 4.6 convert_bitcast_fusion
  12.9 12.0 %copy.37 = bf16[2,16,192,1,2,192]{2,1,0,5,4,3:T(8,128)(2,1)} copy(bf16[2,16,192,1,2,192]{5,1,2,0,4,3:T(8,128)(2,1)} %convert_bitcast_fusion) | data formatting | bytes 9437184 | tf_op jit(solution)/shard_map/convert_element_type | solution.py:29
  24.9 10.7 %reshape.39 = bf16[6144,384]{0,1:T(8,128)(2,1)} reshape(bf16[2,16,192,1,2,192]{2,1,0,5,4,3:T(8,128)(2,1)} %copy.37) | data formatting | bytes 9437184 | tf_op jit(solution)/shard_map/reshape | solution.py:29
  35.6 36.0 %all-gather.2.cloned.1.call-done = bf16[2,192,6144]{2,1,0:T(8,128)(2,1)} async-done(((bf16[2,192,3072]{2,1,0:T(8,128)(2,1)}), bf16[2,192,6144]{2,1,0:T(8,128)(2,1)}) %all-gather.2.cloned.1.call-update) | async-done | bytes 4718608 | tf_op jit(solution)/shard_map/all_gather | solution.py:35
  71.5 3.6 copy.48
  75.2 3.4 copy.34
  78.6 11.3 %gather_fusion = bf16[144,384,128]{2,1,0:T(8,128)(2,1)} fusion(bf16[384,48,128]{2,0,1:T(8,128)(2,1)} %copy.34, s32[1024]{0:T(1024)S(1)} %pad_clamp_fusion), kind=kCustom, calls=%fused_computation | custom fusion | bytes 28312128 | tf_op jit(solution)/shard_map/gather | solution.py:12
  89.9 8.8 bitcast_convert_fusion
  98.7 31.1 %fusion.10 = f32[3072,6144]{1,0:T(8,128)} fusion(bf16[384,3072]{0,1:T(8,128)(2,1)S(1)} %bitcast.66, bf16[6144,384]{0,1:T(8,128)(2,1)} %reshape.39), kind=kOutput, calls=%fused_computation.16 | convolution fusion | flops 14495514624 | bytes 82575360 | tf_op jit(solution)/shard_map/dot_general | solution.py:39
  129.8 699.6 %reduce-scatter.2.cloned.1.call-done = f32[192,6144]{1,0:T(8,128)} async-done(((f32[3072,6144]{1,0:T(8,128)}), f32[192,6144]{1,0:T(8,128)}) %reduce-scatter.2.cloned.1.call-update) | async-done | bytes 4718608 | tf_op jit(solution)/shard_map/reduce_scatter | solution.py:38
  829.4 7.1 reshape.40
  836.5 12.0 %copy.38 = f32[192,2,3072]{0,1,2:T(2,128)} copy(f32[192,2,3072]{2,1,0:T(2,128)} %reshape.40) | data formatting | bytes 9437184 | tf_op jit(solution)/shard_map/reshape | solution.py:46
  848.5 6.8 all-to-all-start
  855.3 5.1 copy.52
  860.3 132.4 %all-to-all-done = f32[192,2,3072]{0,1,2:T(2,128)} async-done(((f32[192,2,3072]{0,1,2:T(2,128)}), f32[192,2,3072]{0,1,2:T(2,128)}, u32[]{:S(2)}, u32[]{:S(2)}) %all-to-all-start) | async-done | bytes 4718624 | tf_op jit(solution)/shard_map/all_to_all | solution.py:48
  992.7 6.1 all-to-all-start.1
  998.8 9.1 copy.39
  1007.9 7.6 all_to_all.19
  1015.5 35.2 %all-to-all-done.1 = f32[192,2,3072]{2,0,1:T(8,128)} async-done(((f32[192,2,3072]{2,0,1:T(8,128)}), f32[192,2,3072]{2,0,1:T(8,128)}, u32[]{:S(2)}, u32[]{:S(2)}) %all-to-all-start.1) | async-done | bytes 4718624 | tf_op jit(solution)/shard_map/all_to_all | solution.py:51
  1050.7 9.2 fusion
  (9 shorter events, 0.1 us)
Async XLA Ops:
  6.5 1.7 copy-start
  6.5 65.0 %all-gather.2.cloned.1.call-start = ((), (), s32[]{:S(2)}) async-start(), calls=%async_computation.3 | async-start | bytes 7077888 | tf_op jit(solution)/shard_map/all_gather | solution.py:35
  7.3 822.2 %reduce-scatter.2.cloned.1.call-start = ((), (), s32[]{:S(2)}) async-start(), calls=%async_computation.4 | async-start | bytes 80216064 | tf_op jit(solution)/shard_map/reduce_scatter | solution.py:38
  848.5 144.2 %all-to-all-start = ((f32[192,2,3072]{0,1,2:T(2,128)}), f32[192,2,3072]{0,1,2:T(2,128)}, u32[]{:S(2)}, u32[]{:S(2)}) async-start(f32[192,2,3072]{0,1,2:T(2,128)} %copy.38), calls=%async_computation.1 | async-start | bytes 12582912 | tf_op jit(solution)/shard_map/all_to_all | solution.py:48
  992.7 58.0 %all-to-all-start.1 = ((f32[192,2,3072]{2,0,1:T(8,128)}), f32[192,2,3072]{2,0,1:T(8,128)}, u32[]{:S(2)}, u32[]{:S(2)}) async-start(f32[192,2,3072]{2,0,1:T(8,128)} %bitcast.63), calls=%async_computation.2 | async-start | bytes 9437184 | tf_op jit(solution)/shard_map/all_to_all | solution.py:51
  1050.7 9.2 copy-start.1
Sparse Core Ops, SparseCore 0:
  8.9 62.6 all-gather.1
  129.9 699.4 reduce-scatter.1
where the time goes:
time: 1070 us
  waiting for transfers between devices  904 us (84%)
  local copies, waits for them, and re-layouts  82 us (8%)
  matrix products  44.6 us (4%)
  between operations  13.4 us (1%)
  starting transfers between devices  12.9 us (1%)
    reduce_scatter x1, waiting for transfers between devices, per_device(): lax.psum_scatter(lax.dot_general(x_stack, spread, (((0,), (1,)), ((), ())...  700 us
    all_to_all x1, waiting for transfers between devices, per_device(): lax.all_to_all(strips, 'row', split_axis=2, concat_axis=0, tiled=True)  132 us
    all_gather x1, waiting for transfers between devices, per_device(): gathered = lax.all_gather(c_matrix, 'col', axis=2, tiled=True)  36 us
    all_to_all x1, waiting for transfers between devices, per_device(): lax.all_to_all(strips, 'col', split_axis=1, concat_axis=1, tiled=True)  35.2 us
    dot_general x1, matrix products, per_device(): lax.dot_general(x_stack, spread, (((0,), (1,)), ((), ())), preferred_elem...  31.1 us
    reshape x3, local copies, waits for them, and re-layouts, per_device(): strips = strips.reshape(stretch_rows, groups, columns)  24.1 us
  transfers between devices with their start and end apart: 4, of which 4 were waited for; matrix products, arithmetic and copies ran while one was open for 4% of the time, Pallas kernels for 0%

commit v1 on v0

v1 whole, which is shorter than its diff:
```python
import functools

import jax
import jax.numpy as jnp
from jax import lax
from jax.experimental import pallas as pl
from jax.experimental.pallas import tpu as pltpu
from jax.sharding import PartitionSpec as P

CONTRACT_LAST = (((1,), (1,)), ((), ()))


def beta_kernel(listed, held, rows_ref, c_ref, b_ref, xt_ref):
    k, j = pl.program_id(0), pl.program_id(1)
    width = b_ref.shape[-1]
    picked = []
    for z in range(listed):
        tile = rows_ref[k, j, z]
        owner = tile // held
        start = pl.multiple_of((tile - owner * held) * width, width)
        picked.append(c_ref[owner, :, pl.ds(start, width)])
    lhs = b_ref[0, 0].reshape(listed * width, width)
    product = lax.dot_general(
        lhs, jnp.concatenate(picked, axis=1), (((0,), (1,)), ((), ())),
        preferred_element_type=jnp.float32,
    )
    xt_ref[0] = product.astype(xt_ref.dtype)


def beta_products(gathered, beta_values, beta_rows):
    pairs, tiles, listed, width, _ = beta_values.shape
    owners, rows, columns = gathered.shape
    return pl.pallas_call(
        functools.partial(beta_kernel, listed, columns // width),
        grid_spec=pltpu.PrefetchScalarGridSpec(
            num_scalar_prefetch=1,
            grid=(pairs, tiles),
            in_specs=[
                pl.BlockSpec((owners, rows, columns), lambda k, j, s: (0, 0, 0)),
                pl.BlockSpec((1, 1, listed, width, width), lambda k, j, s: (k, j, 0, 0, 0)),
            ],
            out_specs=pl.BlockSpec((1, width, rows), lambda k, j, s: (k, j, 0)),
        ),
        out_shape=jax.ShapeDtypeStruct((pairs, tiles * width, rows), jnp.bfloat16),
        compiler_params=pltpu.CompilerParams(vmem_limit_bytes=56 << 20),
        name="beta_products",
    )(beta_rows, gathered, beta_values)


def alpha_kernel(groups, rows_ref, a_ref, x_ref, own_ref, mirror_ref, acc_ref):
    r = pl.program_id(0)
    row_devices = pl.num_programs(0)
    pairs = x_ref.shape[1]
    listed, tile = a_ref.shape[2], a_ref.shape[3]

    @pl.when(r == 0)
    def _():
        acc_ref[...] = jnp.zeros_like(acc_ref)

    for k in range(pairs):
        for g in range(groups):
            x = x_ref[0, k, :, g * tile : (g + 1) * tile]
            slot = k * groups + g
            if tile % 16 == 0:
                product = lax.dot_general(
                    a_ref[0, slot].reshape(listed * tile, tile), x, CONTRACT_LAST,
                    preferred_element_type=jnp.float32,
                )
                for z in range(listed):
                    acc_ref[rows_ref[r, slot, z]] += product[z * tile : (z + 1) * tile]
            else:

                @pl.loop(0, listed)
                def _(z):
                    acc_ref[rows_ref[r, slot, z]] += lax.dot_general(
                        a_ref[0, slot, z], x, CONTRACT_LAST, preferred_element_type=jnp.float32
                    )

    @pl.when(r == row_devices - 1)
    def _():
        count = acc_ref.shape[0] // groups
        for g in range(groups):
            for to in range(count):
                turned = acc_ref[g * count + to].T.astype(own_ref.dtype)
                own_ref[to, :, g * tile : (g + 1) * tile] = turned
                mirror_ref[g, :, to * tile : (to + 1) * tile] = turned


def alpha_products(alpha_all, rows_all, x_strip, groups):
    row_devices, slots, listed, tile, _ = alpha_all.shape
    _, pairs, strip, _ = x_strip.shape
    return pl.pallas_call(
        functools.partial(alpha_kernel, groups),
        grid_spec=pltpu.PrefetchScalarGridSpec(
            num_scalar_prefetch=1,
            grid=(row_devices,),
            in_specs=[
                pl.BlockSpec((1, slots, listed, tile, tile), lambda r, s: (r, 0, 0, 0, 0)),
                pl.BlockSpec((1, pairs, strip, groups * tile), lambda r, s: (r, 0, 0, 0)),
            ],
            out_specs=[
                pl.BlockSpec((row_devices, strip, groups * tile), lambda r, s: (0, 0, 0)),
                pl.BlockSpec((groups, strip, row_devices * tile), lambda r, s: (0, 0, 0)),
            ],
            scratch_shapes=[pltpu.VMEM((groups * row_devices, tile, strip), jnp.float32)],
        ),
        out_shape=[
            jax.ShapeDtypeStruct((row_devices, strip, groups * tile), jnp.bfloat16),
            jax.ShapeDtypeStruct((groups, strip, row_devices * tile), jnp.bfloat16),
        ],
        compiler_params=pltpu.CompilerParams(vmem_limit_bytes=56 << 20),
        name="alpha_products",
    )(rows_all, alpha_all, x_strip)


def final_kernel(own_ref, mirror_ref, gaps_ref, out_ref):
    own = own_ref[...].astype(jnp.float32).T
    out_ref[...] = (own + mirror_ref[...].astype(jnp.float32)) / gaps_ref[...]


def final(own, mirror, gaps):
    rows, columns = gaps.shape
    block = next(n for n in (384, 256, 128) if columns % n == 0)
    wide = pl.BlockSpec((rows, block), lambda i: (0, i))
    return pl.pallas_call(
        final_kernel,
        grid=(columns // block,),
        in_specs=[pl.BlockSpec((block, rows), lambda i: (i, 0)), wide, wide],
        out_specs=wide,
        out_shape=jax.ShapeDtypeStruct((rows, columns), jnp.float32),
        name="final",
    )(own, mirror, gaps)


def per_device(c_matrix, beta_values, beta_rows, alpha_values, alpha_rows, gaps):
    row_devices = lax.axis_size("row")
    groups, stretch, columns = c_matrix.shape
    pairs, _, _, listed, tile, _ = alpha_values.shape
    rows_all = lax.all_gather(alpha_rows[:, :, 0].reshape(pairs * groups, listed), "row")
    gathered = lax.all_gather(c_matrix.reshape(groups * stretch, columns), "col")
    alpha_all = lax.all_gather(
        alpha_values[:, :, 0].reshape(pairs * groups, listed, tile, tile), "row"
    )
    xt = beta_products(gathered, beta_values, beta_rows)
    xt = jnp.moveaxis(xt.reshape(pairs, row_devices, stretch, groups * stretch), 1, 0)
    x_strip = lax.all_to_all(xt, "row", 0, 0)
    own, mirror = alpha_products(alpha_all, rows_all, x_strip, groups)
    own = lax.all_to_all(own, "row", 0, 0)
    mirror = lax.all_to_all(mirror, "col", 0, 0)
    out = final(
        own.reshape(columns, groups * stretch),
        mirror.reshape(groups * stretch, columns),
        gaps.reshape(groups * stretch, columns),
    )
    return out.reshape(gaps.shape)


def solution(mesh):
    placed = (
        P(None, "row", "col"),
        P(None, "col", None, None, None),
        P(None, "col", None),
        P(None, None, "row", None, None, None),
        P(None, None, "row", None),
        P(None, "row", "col"),
    )
    return jax.shard_map(
        per_device, mesh=mesh, in_specs=placed, out_specs=P(None, "row", "col"), check_vma=False
    )
```

time: 1070 us -> 345 us (0.32)
  waiting for transfers between devices: 904 us -> 64.3 us
  blocking collectives: 0 us -> 207 us
  local copies, waits for them, and re-layouts: 82 us -> 2.08 us
  Pallas kernels: 0 us -> 47.2 us
  matrix products: 44.6 us -> 0 us
    reduce_scatter x1 -> x0, waiting for transfers between devices: 700 us -> none  [per_device(): lax.psum_scatter(lax.dot_general(x_stack, spread, (((0,), (1,)), ((), ())...]
    all_to_all x2 -> x1, waiting for transfers between devices: 168 us -> 0.01 us  [per_device(): x_strip = lax.all_to_all(xt, 'row', 0, 0)]
    all_gather x0 -> x1, blocking collectives: none -> 115 us  [per_device(): lax.all_gather(alpha_rows[:, :, 0].reshape(pairs * groups, listed), 'row')]
    all_to_all x0 -> x2, blocking collectives: none -> 92.1 us  [the longest x1 59.6 us: per_device(): own = lax.all_to_all(own, 'row', 0, 0)]
    pallas_call x0 -> x3, Pallas kernels: none -> 47.2 us  [the longest x1 19.9 us: beta_products(): pl.pallas_call(functools.partial(beta_kernel, listed, columns // width),...]
    dot_general x3 -> x0, matrix products: 44.6 us -> none  [the longest x1 31.1 us: per_device(): lax.dot_general(x_stack, spread, (((0,), (1,)), ((), ())), preferred_elem...]
    reshape x5 -> x0, local copies, waits for them, and re-layouts: 38.2 us -> none  [the longest x3 24.1 us: per_device(): strips = strips.reshape(stretch_rows, groups, columns)]
    all_gather x1 -> x2, waiting for transfers between devices: 36 us -> 62.9 us  [the longest x1 62.8 us: per_device(): lax.all_gather(c_matrix.reshape(groups * stretch, columns), 'col')]
  transfers between devices with their start and end apart: 4 -> 3, of which waited for: 4 -> 1; matrix products, arithmetic and copies ran while one was open for 4% -> 0% of each run, Pallas kernels for 0% -> 6%
where the time goes in v1:
time: 345 us; the launch traced here: 341 us
  blocking collectives  207 us (60%)
  waiting for transfers between devices  64.3 us (19%)
  Pallas kernels  47.2 us (14%)
  between operations  13.4 us (4%)
  starting transfers between devices  6.72 us (2%)
    all_gather x1, blocking collectives, per_device(): lax.all_gather(alpha_rows[:, :, 0].reshape(pairs * groups, listed), 'row')  115 us
    all_gather x1, waiting for transfers between devices, per_device(): lax.all_gather(c_matrix.reshape(groups * stretch, columns), 'col')  62.8 us
    all_to_all x1, blocking collectives, per_device(): own = lax.all_to_all(own, 'row', 0, 0)  59.6 us
    all_to_all x1, blocking collectives, per_device(): mirror = lax.all_to_all(mirror, 'col', 0, 0)  32.5 us
    pallas_call x1, Pallas kernels, beta_products(): pl.pallas_call(functools.partial(beta_kernel, listed, columns // width),...  19.9 us
    pallas_call x1, Pallas kernels, alpha_products(): pl.pallas_call(functools.partial(alpha_kernel, groups), grid_spec=pltpu.P...  18.9 us
    pallas_call x1, Pallas kernels, final(): pl.pallas_call(final_kernel, grid=(columns // block,), in_specs=[pl.Block...  8.34 us
  transfers between devices with their start and end apart: 3, of which 1 were waited for; matrix products, arithmetic and copies ran while one was open for 0% of the time, Pallas kernels for 6%

profile of v1, /device:TPU:15, one launch (start us, length us, event | category | flops | bytes accessed | tf_op | source)
XLA Modules:
  0.0 340.5 jit_solution(11735596421071150701)
XLA Ops:
  6.5 0.0 copy-start.2
  6.5 0.0 all-gather.5.cloned.1.call-start
  6.5 0.7 all-gather.5.cloned.1.call-update
  7.3 0.0 all-gather.7.cloned.1.call-start
  7.3 0.7 all-gather.7.cloned.1.call-update
  8.0 0.0 copy-done.2
  8.0 0.7 copy.13.rows_ref
  8.7 62.8 %all-gather.5.cloned.1.call-done.c_ref = bf16[2,384,3072]{2,1,0:T(8,128)(2,1)} async-done(((bf16[1,384,3072]{2,1,0:T(8,128)(2,1)}), bf16[2,384,3072]{2,1,0:T(8,128)(2,1)}) %all-gather.5.cloned.1.call-update) | async-done | bytes 4718608 | tf_op jit(solution)/shard_map/all_gather | solution.py:140
  71.5 19.9 %beta_products.1 = bf16[1,3072,384]{2,1,0:T(8,128)(2,1)} custom-call(s32[1,24,6]{2,1,0:T(8,128)} %copy.13.rows_ref, bf16[2,384,3072]{2,1,0:T(8,128)(2,1)} %all-gather.5.cloned.1.call-done.c_ref, bf16[1,24,6,128,128]{4,3,2,1,0:T(8,128)(2,1)} %b_ref.1), custom_call_target="tpu_custom_call" | custom-call | tf_op jit(solution)/shard_map/beta_products/pallas_call | solution.py:33
  91.5 0.0 copy-start.3
  91.5 6.7 %all-to-all-start = ((bf16[16,1,192,384]{3,2,1,0:T(8,128)(2,1)}), bf16[16,1,192,384]{3,2,1,0:T(8,128)(2,1)S(1)}, u32[]{:S(2)}, u32[]{:S(2)}) async-start(bf16[16,1,192,384]{3,2,1,0:T(8,128)(2,1)} %bitcast.12), calls=%async_computation | async-start | bytes 4718592 | tf_op jit(solution)/shard_map/all_to_all | solution.py:146
  98.2 0.0 copy-done.3
  98.2 114.8 %all-gather = s32[16,2,1,4]{3,1,2,0:T(2,128)} all-gather(s32[1,2,1,4]{3,1,2,0:T(2,128)S(1)} %bitcast.16), channel_id=2, replica_groups=mesh['row'=16,'col'=2] {'row'}, dimensions={0}, use_global_device_ids=true | all-gather | bytes 544 | tf_op jit(solution)/shard_map/all_gather | solution.py:139
  213.0 0.0 all-to-all-done.x_ref
  213.0 0.0 copy-start
  213.0 0.0 all-gather.7.cloned.1.call-done
  213.0 1.4 copy-done
  214.4 18.9 %alpha_products.1 = (bf16[16,192,384]{2,1,0:T(8,128)(2,1)}, bf16[2,192,3072]{2,1,0:T(8,128)(2,1)}) custom-call(s32[16,2,4]{2,1,0:T(2,128)} %bitcast.15, bf16[16,2,4,192,192]{4,3,2,1,0:T(8,128)(2,1)} %bitcast.9, bf16[16,1,192,384]{3,2,1,0:T(8,128)(2,1)} %copy-done), custom_call_target="tpu_custom_call" | custom-call | tf_op jit(solution)/shard_map/alpha_products/pallas_call | solution.py:92
  233.3 0.0 copy-start.1
  233.3 32.5 %all_to_all.15 = bf16[2,192,3072]{2,1,0:T(8,128)(2,1)} all-to-all(bf16[2,192,3072]{2,1,0:T(8,128)(2,1)} %get-tuple-element.8), channel_id=1, replica_groups=mesh['row'=16,'col'=2] {'col'}, dimensions={0} | all-to-all | bytes 4718592 | tf_op jit(solution)/shard_map/all_to_all | solution.py:149
  265.8 0.0 copy-done.1
  265.8 59.6 %all_to_all.16 = bf16[16,192,384]{2,1,0:T(8,128)(2,1)} all-to-all(bf16[16,192,384]{2,1,0:T(8,128)(2,1)S(1)} %copy-done.1), channel_id=1, replica_groups=mesh['row'=16,'col'=2] {'row'}, dimensions={0} | all-to-all | bytes 4718592 | tf_op jit(solution)/shard_map/all_to_all | solution.py:148
  325.3 8.3 %final.1 = f32[384,3072]{1,0:T(8,128)} custom-call(bf16[3072,384]{1,0:T(8,128)(2,1)} %bitcast.11, bf16[384,3072]{1,0:T(8,128)(2,1)} %bitcast.10, f32[384,3072]{1,0:T(8,128)} %bitcast.13), custom_call_target="tpu_custom_call" | custom-call | tf_op jit(solution)/shard_map/final/pallas_call | solution.py:125
Async XLA Ops:
  6.5 1.5 copy-start.2
  6.5 65.0 %all-gather.5.cloned.1.call-start = ((), (), s32[]{:S(2)}) async-start(), calls=%async_computation.3 | async-start | bytes 7077888 | tf_op jit(solution)/shard_map/all_gather | solution.py:140
  7.3 205.7 %all-gather.7.cloned.1.call-start = ((), (), s32[]{:S(2)}) async-start(), calls=%async_computation.4 | async-start | bytes 13369344 | tf_op jit(solution)/shard_map/all_gather | solution.py:141
  91.5 6.7 %copy-start.3 = (s32[1,2,1,4]{3,2,1,0:T(1,128)S(1)}, s32[1,2,1,4]{3,2,1,0:T(1,128)}, u32[]{:S(2)}) copy-start(s32[1,2,1,4]{3,2,1,0:T(1,128)} %param.10) | copy-start | bytes 100
  91.5 121.5 %all-to-all-start = ((bf16[16,1,192,384]{3,2,1,0:T(8,128)(2,1)}), bf16[16,1,192,384]{3,2,1,0:T(8,128)(2,1)S(1)}, u32[]{:S(2)}, u32[]{:S(2)}) async-start(bf16[16,1,192,384]{3,2,1,0:T(8,128)(2,1)} %bitcast.12), calls=%async_computation | async-start | bytes 4718592 | tf_op jit(solution)/shard_map/all_to_all | solution.py:146
  213.0 1.4 copy-start
  233.3 32.5 %copy-start.1 = (bf16[16,192,384]{2,1,0:T(8,128)(2,1)S(1)}, bf16[16,192,384]{2,1,0:T(8,128)(2,1)}, u32[]{:S(2)}) copy-start(bf16[16,192,384]{2,1,0:T(8,128)(2,1)} %get-tuple-element.7) | copy-start | bytes 7077892
Sparse Core Ops, SparseCore 0:
  8.9 62.6 all-gather.4
  73.8 137.4 all-gather.6

commit v2 on v1

--- a/solution.py
+++ b/solution.py
@@ -50,7 +50,7 @@
 def alpha_kernel(groups, rows_ref, a_ref, x_ref, own_ref, mirror_ref, acc_ref):
     r = pl.program_id(0)
     row_devices = pl.num_programs(0)
-    pairs = x_ref.shape[1]
+    pairs = x_ref.shape[2]
     listed, tile = a_ref.shape[2], a_ref.shape[3]
 
     @pl.when(r == 0)
@@ -58,8 +58,10 @@
         acc_ref[...] = jnp.zeros_like(acc_ref)
 
     for k in range(pairs):
+        parts = [x_ref[c, 0, k] for c in range(x_ref.shape[0])]
+        merged = jnp.concatenate(parts, axis=1) if len(parts) > 1 else parts[0]
         for g in range(groups):
-            x = x_ref[0, k, :, g * tile : (g + 1) * tile]
+            x = merged[:, g * tile : (g + 1) * tile]
             slot = k * groups + g
             if tile % 16 == 0:
                 product = lax.dot_general(
@@ -88,7 +90,7 @@
 
 def alpha_products(alpha_all, rows_all, x_strip, groups):
     row_devices, slots, listed, tile, _ = alpha_all.shape
-    _, pairs, strip, _ = x_strip.shape
+    chunks, _, pairs, strip, chunk = x_strip.shape
     return pl.pallas_call(
         functools.partial(alpha_kernel, groups),
         grid_spec=pltpu.PrefetchScalarGridSpec(
@@ -96,7 +98,7 @@
             grid=(row_devices,),
             in_specs=[
                 pl.BlockSpec((1, slots, listed, tile, tile), lambda r, s: (r, 0, 0, 0, 0)),
-                pl.BlockSpec((1, pairs, strip, groups * tile), lambda r, s: (r, 0, 0, 0)),
+                pl.BlockSpec((chunks, 1, pairs, strip, chunk), lambda r, s: (0, r, 0, 0, 0)),
             ],
             out_specs=[
                 pl.BlockSpec((row_devices, strip, groups * tile), lambda r, s: (0, 0, 0)),
@@ -132,21 +134,256 @@
     )(own, mirror, gaps)
 
 
+def greet(axes):
+    barrier = pltpu.get_barrier_semaphore()
+    total = 0
+    for axis in axes:
+        size, me = lax.axis_size(axis), lax.axis_index(axis)
+        total += size - 1
+
+        @pl.loop(1, size)
+        def _(off):
+            pl.semaphore_signal(
+                barrier, inc=1, device_id={axis: lax.rem(me + off, size)},
+                device_id_type=pl.DeviceIdType.MESH,
+            )
+
+    pl.semaphore_wait(barrier, total)
+
+
+def remote(src, dst, send_sem, recv_sem, axis, peer):
+    return pltpu.make_async_remote_copy(
+        src_ref=src, dst_ref=dst, send_sem=send_sem, recv_sem=recv_sem,
+        device_id={axis: peer}, device_id_type=pl.DeviceIdType.MESH,
+    )
+
+
+def spread_kernel(chunks, rows_ref, c_ref, b_ref, list_ref, x_ref, lists_ref, *scratch):
+    held, sent = scratch[:chunks], scratch[chunks : 2 * chunks]
+    local_sem, c_send, c_recv, x_send, x_recv, own_sem, l_send, l_recv, l_own = scratch[2 * chunks :]
+    row_devices, row = lax.axis_size("row"), lax.axis_index("row")
+    col_devices, col = lax.axis_size("col"), lax.axis_index("col")
+    pairs, tiles, listed, width, _ = b_ref.shape
+    per_owner, rows, _ = c_ref.shape
+    chunk = rows // chunks
+    strip = per_owner * width // row_devices
+
+    def own_c(c):
+        return pltpu.make_async_copy(
+            c_ref.at[:, pl.ds(c * chunk, chunk)], held[c].at[pl.ds(col * per_owner, per_owner)],
+            local_sem.at[c],
+        )
+
+    def send_c(c, off):
+        return remote(
+            c_ref.at[:, pl.ds(c * chunk, chunk)], held[c].at[pl.ds(col * per_owner, per_owner)],
+            c_send.at[c, off - 1], c_recv.at[c, off - 1], "col", lax.rem(col + off, col_devices),
+        )
+
+    def send_x(c, off):
+        peer = lax.rem(row + off, row_devices)
+        start = pl.multiple_of(peer * strip, 16)
+        return remote(
+            sent[c].at[:, pl.ds(start, strip), :], x_ref.at[c, row], x_send.at[c, off - 1],
+            x_recv.at[c, off - 1], "row", peer,
+        )
+
+    def own_x(c):
+        start = pl.multiple_of(row * strip, 16)
+        return pltpu.make_async_copy(
+            sent[c].at[:, pl.ds(start, strip), :], x_ref.at[c, row], own_sem.at[c]
+        )
+
+    def send_list(off):
+        return remote(
+            list_ref, lists_ref.at[row], l_send.at[off - 1], l_recv.at[off - 1], "row",
+            lax.rem(row + off, row_devices),
+        )
+
+    own_list = pltpu.make_async_copy(list_ref, lists_ref.at[row], l_own)
+    for c in range(chunks):
+        own_c(c).start()
+    own_list.start()
+    greet(("row", "col"))
+    for c in range(chunks):
+        for off in range(1, col_devices):
+            send_c(c, off).start()
+
+    @pl.loop(1, row_devices)
+    def _(off):
+        send_list(off).start()
+
+    for c in range(chunks):
+        own_c(c).wait()
+        for off in range(1, col_devices):
+            send_c(c, off).wait_recv()
+
+        @pl.loop(0, tiles)
+        def _(j):
+            for k in range(pairs):
+                picked = [held[c][rows_ref[k, j, z]] for z in range(listed)]
+                product = lax.dot_general(
+                    b_ref[k, j].reshape(listed * width, width), jnp.concatenate(picked, axis=1),
+                    (((0,), (1,)), ((), ())), preferred_element_type=jnp.float32,
+                )
+                sent[c][k, pl.ds(pl.multiple_of(j * width, width), width), :] = product.astype(
+                    jnp.bfloat16
+                )
+
+        @pl.loop(1, row_devices)
+        def _(off):
+            send_x(c, off).start()
+
+        own_x(c).start()
+
+    own_list.wait()
+
+    @pl.loop(1, row_devices)
+    def _(off):
+        send_list(off).wait()
+
+    for c in range(chunks):
+        own_x(c).wait()
+        for off in range(1, col_devices):
+            send_c(c, off).wait_send()
+
+        @pl.loop(1, row_devices)
+        def _(off):
+            send_x(c, off).wait()
+
+
+def spread(c_matrix, beta_values, beta_rows, alpha_list, row_devices, col_devices, chunk):
+    rows, columns = c_matrix.shape
+    pairs, _, _, width, _ = beta_values.shape
+    c_tiles = jnp.moveaxis(c_matrix.reshape(rows, columns // width, width), 1, 0)
+    strip, chunks = columns // row_devices, rows // chunk
+    dma = pltpu.SemaphoreType.DMA
+    anywhere = pl.BlockSpec(memory_space=pl.ANY)
+    return pl.pallas_call(
+        functools.partial(spread_kernel, chunks),
+        in_specs=[
+            pl.BlockSpec(memory_space=pltpu.SMEM), anywhere,
+            pl.BlockSpec(memory_space=pltpu.VMEM), pl.BlockSpec(memory_space=pltpu.VMEM),
+        ],
+        out_specs=[anywhere, anywhere],
+        out_shape=[
+            jax.ShapeDtypeStruct((chunks, row_devices, pairs, strip, chunk), jnp.bfloat16),
+            jax.ShapeDtypeStruct((row_devices,) + alpha_list.shape, jnp.int32),
+        ],
+        scratch_shapes=[pltpu.VMEM((col_devices * columns // width, chunk, width), jnp.bfloat16)] * chunks
+        + [pltpu.VMEM((pairs, columns, chunk), jnp.bfloat16)] * chunks
+        + [
+            dma((chunks,)), dma((chunks, col_devices - 1)), dma((chunks, col_devices - 1)),
+            dma((chunks, row_devices - 1)), dma((chunks, row_devices - 1)), dma((chunks,)),
+            dma((row_devices - 1,)), dma((row_devices - 1,)), dma,
+        ],
+        compiler_params=pltpu.CompilerParams(
+            collective_id=0, has_side_effects=True, vmem_limit_bytes=56 << 20
+        ),
+        cost_estimate=pl.CostEstimate(
+            flops=1 << 37, bytes_accessed=1 << 28, transcendentals=0
+        ),
+        name="spread",
+    )(beta_rows, c_tiles, beta_values, alpha_list)
+
+
+def exchange_kernel(own_ref, mirror_ref, own_out, mirror_out, o_send, o_recv, m_send, m_recv, sems):
+    row_devices, row = lax.axis_size("row"), lax.axis_index("row")
+    col_devices, col = lax.axis_size("col"), lax.axis_index("col")
+
+    def send_own(off):
+        peer = lax.rem(row + off, row_devices)
+        return remote(
+            own_ref.at[peer], own_out.at[row], o_send.at[off - 1], o_recv.at[off - 1], "row", peer
+        )
+
+    def send_mirror(off):
+        peer = lax.rem(col + off, col_devices)
+        return remote(
+            mirror_ref.at[peer], mirror_out.at[col], m_send.at[off - 1], m_recv.at[off - 1],
+            "col", peer,
+        )
+
+    stay_own = pltpu.make_async_copy(own_ref.at[row], own_out.at[row], sems.at[0])
+    stay_mirror = pltpu.make_async_copy(mirror_ref.at[col], mirror_out.at[col], sems.at[1])
+    greet(("row", "col"))
+
+    @pl.loop(1, col_devices)
+    def _(off):
+        send_mirror(off).start()
+
+    @pl.loop(1, row_devices)
+    def _(off):
+        send_own(off).start()
+
+    stay_own.start()
+    stay_mirror.start()
+    stay_own.wait()
+    stay_mirror.wait()
+
+    @pl.loop(1, row_devices)
+    def _(off):
+        send_own(off).wait()
+
+    @pl.loop(1, col_devices)
+    def _(off):
+        send_mirror(off).wait()
+
+
+def exchange(own, mirror):
+    dma = pltpu.SemaphoreType.DMA
+    anywhere = pl.BlockSpec(memory_space=pl.ANY)
+    local = pl.BlockSpec(memory_space=pltpu.VMEM)
+    row_devices, col_devices = own.shape[0], mirror.shape[0]
+    return pl.pallas_call(
+        exchange_kernel,
+        in_specs=[local, local],
+        out_specs=[anywhere, anywhere],
+        out_shape=[
+            jax.ShapeDtypeStruct(own.shape, own.dtype),
+            jax.ShapeDtypeStruct(mirror.shape, mirror.dtype),
+        ],
+        scratch_shapes=[
+            dma((row_devices - 1,)), dma((row_devices - 1,)),
+            dma((col_devices - 1,)), dma((col_devices - 1,)), dma((2,)),
+        ],
+        compiler_params=pltpu.CompilerParams(
+            collective_id=1, has_side_effects=True, vmem_limit_bytes=56 << 20
+        ),
+        name="exchange",
+    )(own, mirror)
+
+
 def per_device(c_matrix, beta_values, beta_rows, alpha_values, alpha_rows, gaps):
-    row_devices = lax.axis_size("row")
+    row_devices, col_devices = lax.axis_size("row"), lax.axis_size("col")
     groups, stretch, columns = c_matrix.shape
     pairs, _, _, listed, tile, _ = alpha_values.shape
-    rows_all = lax.all_gather(alpha_rows[:, :, 0].reshape(pairs * groups, listed), "row")
-    gathered = lax.all_gather(c_matrix.reshape(groups * stretch, columns), "col")
+    rows, chunk = groups * stretch, beta_values.shape[-1]
+    c_rows = c_matrix.reshape(rows, columns)
     alpha_all = lax.all_gather(
         alpha_values[:, :, 0].reshape(pairs * groups, listed, tile, tile), "row"
     )
-    xt = beta_products(gathered, beta_values, beta_rows)
-    xt = jnp.moveaxis(xt.reshape(pairs, row_devices, stretch, groups * stretch), 1, 0)
-    x_strip = lax.all_to_all(xt, "row", 0, 0)
+    alpha_list = alpha_rows[:, :, 0].reshape(pairs * groups, listed)
+    own_kernels = stretch % 16 == 0 and rows % chunk == 0
+    if own_kernels:
+        entries = alpha_list.size
+        padded = jnp.pad(alpha_list.reshape(-1), (0, -entries % 1024)).reshape(-1, 128)
+        x_strip, rows_all = spread(
+            c_rows, beta_values, beta_rows, padded, row_devices, col_devices, chunk
+        )
+        rows_all = rows_all.reshape(row_devices, -1)[:, :entries]
+        rows_all = rows_all.reshape(row_devices, pairs * groups, listed)
+    else:
+        rows_all = lax.all_gather(alpha_list, "row")
+        xt = beta_products(lax.all_gather(c_rows, "col"), beta_values, beta_rows)
+        xt = jnp.moveaxis(xt.reshape(pairs, row_devices, stretch, rows), 1, 0)
+        x_strip = lax.all_to_all(xt, "row", 0, 0)[None]
     own, mirror = alpha_products(alpha_all, rows_all, x_strip, groups)
-    own = lax.all_to_all(own, "row", 0, 0)
-    mirror = lax.all_to_all(mirror, "col", 0, 0)
+    if own_kernels:
+        own, mirror = exchange(own, mirror)
+    else:
+        own = lax.all_to_all(own, "row", 0, 0)
+        mirror = lax.all_to_all(mirror, "col", 0, 0)
     out = final(
         own.reshape(columns, groups * stretch),
         mirror.reshape(groups * stretch, columns),

time: 345 us -> 245 us (0.71); the launches traced: 341 us -> 244 us
  blocking collectives: 207 us -> 0 us
  Pallas kernels: 47.2 us -> 219 us
  waiting for transfers between devices: 64.3 us -> 2.16 us
  starting transfers between devices: 6.72 us -> 0.01 us
  local copies, waits for them, and re-layouts: 2.08 us -> 8.46 us
    pallas_call x1 -> x2, Pallas kernels: 19.9 us -> 192 us  [the longest x1 130 us: spread(): pl.pallas_call(functools.partial(spread_kernel, chunks), in_specs=[pl.Blo...]
    all_gather x1 -> x0, blocking collectives: 115 us -> none  [per_device(): lax.all_gather(alpha_rows[:, :, 0].reshape(pairs * groups, listed), 'row')]
    all_to_all x2 -> x0, blocking collectives: 92.1 us -> none  [the longest x1 59.6 us: per_device(): own = lax.all_to_all(own, 'row', 0, 0)]
    all_gather x1 -> x0, waiting for transfers between devices: 62.8 us -> none  [per_device(): lax.all_gather(c_matrix.reshape(groups * stretch, columns), 'col')]
    all_to_all x1 -> x0, starting transfers between devices: 6.68 us -> none  [per_device(): x_strip = lax.all_to_all(xt, 'row', 0, 0)]
  transfers between devices with their start and end apart: 3 -> 1, of which waited for: 1 -> 1; matrix products, arithmetic and copies ran while one was open for 0% -> 4% of each run, Pallas kernels for 6% -> 53%
where the time goes in v2:
time: 245 us; the launch traced here: 244 us
  Pallas kernels  219 us (89%)
  between operations  13.4 us (5%)
  local copies, waits for them, and re-layouts  8.46 us (3%)
    pallas_call x1, Pallas kernels, spread(): pl.pallas_call(functools.partial(spread_kernel, chunks), in_specs=[pl.Blo...  130 us
    pallas_call x1, Pallas kernels, exchange(): pl.pallas_call(exchange_kernel, in_specs=[local, local], out_specs=[anywh...  61.8 us
    pallas_call x1, Pallas kernels, alpha_products(): pl.pallas_call(functools.partial(alpha_kernel, groups), grid_spec=pltpu.P...  19 us
    pallas_call x1, Pallas kernels, final(): pl.pallas_call(final_kernel, grid=(columns // block,), in_specs=[pl.Block...  8.36 us
  transfers between devices with their start and end apart: 1, of which 1 were waited for; matrix products, arithmetic and copies ran while one was open for 4% of the time, Pallas kernels for 53%

profile of v2, /device:TPU:15, one launch (start us, length us, event | category | flops | bytes accessed | tf_op | source)
XLA Modules:
  0.0 244.3 jit_solution(6831331689350816124)
XLA Ops:
  6.5 0.0 all-gather.3.cloned.1.call-start
  6.5 0.7 all-gather.3.cloned.1.call-update
  7.3 0.5 broadcast.5
  7.8 1.3 reduce.3
  9.1 0.1 reshape_reshape_squeeze.3
  9.2 1.4 copy.17.rows_ref
  10.6 2.2 copy.21
  12.8 1.9 copy.23
  14.7 0.6 pad_bitcast_fusion.list_ref
  15.3 129.7 %spread.1 = (bf16[3,16,1,192,128]{4,3,2,1,0:T(8,128)(2,1)}, s32[16,8,128]{2,1,0:T(8,128)}) custom-call(s32[1,24,6]{2,1,0:T(8,128)} %copy.17.rows_ref, bf16[24,384,128]{2,1,0:T(8,128)(2,1)} %bitcast.21, bf16[1,24,6,128,128]{4,3,2,1,0:T(8,128)(2,1)} %b_ref.1, s32[8,128]{1,0:T(8,128)} %pad_bitcast_fusion.list_ref), custom_call_target="tpu_custom_call" | custom-call | flops 137438953472 | bytes 268435456 | tf_op jit(solution)/shard_map/spread/pallas_call | solution.py:262
  145.0 1.0 copy.20
  146.1 0.7 copy.19.rows_ref
  146.8 1.4 all-gather.3.cloned.1.call-done
  148.2 19.0 %alpha_products.1 = (bf16[16,192,384]{2,1,0:T(8,128)(2,1)}, bf16[2,192,3072]{2,1,0:T(8,128)(2,1)}) custom-call(s32[16,2,4]{2,1,0:T(2,128)} %copy.19.rows_ref, bf16[16,2,4,192,192]{4,3,2,1,0:T(8,128)(2,1)} %bitcast.15, bf16[3,16,1,192,128]{4,3,2,1,0:T(8,128)(2,1)} %get-tuple-element.12.x_ref), custom_call_target="tpu_custom_call" | custom-call | tf_op jit(solution)/shard_map/alpha_products/pallas_call | solution.py:94
  167.2 61.8 %exchange.1 = (bf16[16,192,384]{2,1,0:T(8,128)(2,1)}, bf16[2,192,3072]{2,1,0:T(8,128)(2,1)}) custom-call(bf16[16,192,384]{2,1,0:T(8,128)(2,1)} %get-tuple-element.13.own_ref, bf16[2,192,3072]{2,1,0:T(8,128)(2,1)} %get-tuple-element.14.mirror_ref), custom_call_target="tpu_custom_call" | custom-call | tf_op jit(solution)/shard_map/exchange/pallas_call | solution.py:338
  229.1 8.4 %final.1 = f32[384,3072]{1,0:T(8,128)} custom-call(bf16[3072,384]{1,0:T(8,128)(2,1)} %bitcast.18, bf16[384,3072]{1,0:T(8,128)(2,1)} %bitcast.19, f32[384,3072]{1,0:T(8,128)} %bitcast.17), custom_call_target="tpu_custom_call" | custom-call | tf_op jit(solution)/shard_map/final/pallas_call | solution.py:127
  (1 shorter events, 0.0 us)
Async XLA Ops:
  6.5 141.7 %all-gather.3.cloned.1.call-start = ((), (), s32[]{:S(2)}) async-start(), calls=%async_computation | async-start | bytes 13369344 | tf_op jit(solution)/shard_map/all_gather | solution.py:363
Sparse Core Ops, SparseCore 0:
  9.6 138.5 all-gather.2

commit v3 on v2

--- a/solution.py
+++ b/solution.py
@@ -47,11 +47,34 @@
     )(beta_rows, gathered, beta_values)
 
 
+def pack_alpha(tiles):
+    count, listed, tile, _ = tiles.shape
+    flat = tiles.reshape(count * listed * tile, tile)
+    half, whole = flat.shape[0] // 2, tile // 128
+    parts = [flat[:, i * 128 : (i + 1) * 128] for i in range(whole)]
+    parts.append(jnp.concatenate([flat[:half, whole * 128 :], flat[half:, whole * 128 :]], axis=1))
+    return jnp.concatenate(parts, axis=0)
+
+
+def packed_product(a_ref, slot, slots, listed, tile, x):
+    size, whole = listed * tile, tile // 128
+    parts = [a_ref[0, pl.ds(i * slots * size + slot * size, size), :] for i in range(whole)]
+    parts.append(a_ref[0, pl.ds(whole * slots * size + slot % (slots // 2) * size, size), :])
+    blank = jnp.zeros((x.shape[0], 64), x.dtype)
+    tail = [x[:, whole * 128 :], blank]
+    if slot >= slots // 2:
+        tail = tail[::-1]
+    wide = jnp.concatenate([x[:, : whole * 128]] + tail, axis=1)
+    return lax.dot_general(
+        jnp.concatenate(parts, axis=1), wide, CONTRACT_LAST, preferred_element_type=jnp.float32
+    )
+
+
 def alpha_kernel(groups, rows_ref, a_ref, x_ref, own_ref, mirror_ref, acc_ref):
     r = pl.program_id(0)
     row_devices = pl.num_programs(0)
     pairs = x_ref.shape[2]
-    listed, tile = a_ref.shape[2], a_ref.shape[3]
+    listed, tile = rows_ref.shape[2], acc_ref.shape[1]
 
     @pl.when(r == 0)
     def _():
@@ -63,11 +86,8 @@
         for g in range(groups):
             x = merged[:, g * tile : (g + 1) * tile]
             slot = k * groups + g
-            if tile % 16 == 0:
-                product = lax.dot_general(
-                    a_ref[0, slot].reshape(listed * tile, tile), x, CONTRACT_LAST,
-                    preferred_element_type=jnp.float32,
-                )
+            if len(a_ref.shape) == 3:
+                product = packed_product(a_ref, slot, pairs * groups, listed, tile, x)
                 for z in range(listed):
                     acc_ref[rows_ref[r, slot, z]] += product[z * tile : (z + 1) * tile]
             else:
@@ -89,7 +109,8 @@
 
 
 def alpha_products(alpha_all, rows_all, x_strip, groups):
-    row_devices, slots, listed, tile, _ = alpha_all.shape
+    row_devices, rest = alpha_all.shape[0], alpha_all.shape[1:]
+    tile = x_strip.shape[0] * x_strip.shape[-1] // groups
     chunks, _, pairs, strip, chunk = x_strip.shape
     return pl.pallas_call(
         functools.partial(alpha_kernel, groups),
@@ -97,7 +118,7 @@
             num_scalar_prefetch=1,
             grid=(row_devices,),
             in_specs=[
-                pl.BlockSpec((1, slots, listed, tile, tile), lambda r, s: (r, 0, 0, 0, 0)),
+                pl.BlockSpec((1,) + rest, lambda r, s: (r,) + (0,) * len(rest)),
                 pl.BlockSpec((chunks, 1, pairs, strip, chunk), lambda r, s: (0, r, 0, 0, 0)),
             ],
             out_specs=[
@@ -158,9 +179,10 @@
     )
 
 
-def spread_kernel(chunks, rows_ref, c_ref, b_ref, list_ref, x_ref, lists_ref, *scratch):
+def spread_kernel(chunks, rows_ref, c_ref, b_ref, list_ref, a_ref, x_ref, lists_ref, all_ref, *scratch):
     held, sent = scratch[:chunks], scratch[chunks : 2 * chunks]
-    local_sem, c_send, c_recv, x_send, x_recv, own_sem, l_send, l_recv, l_own = scratch[2 * chunks :]
+    (local_sem, c_send, c_recv, x_send, x_recv, own_sem, l_send, l_recv, l_own, up_send, up_recv,
+     down_send, down_recv, y_send, y_recv, core_send, core_recv, a_own) = scratch[2 * chunks :]
     row_devices, row = lax.axis_size("row"), lax.axis_index("row")
     col_devices, col = lax.axis_size("col"), lax.axis_index("col")
     pairs, tiles, listed, width, _ = b_ref.shape
@@ -200,20 +222,100 @@
             lax.rem(row + off, row_devices),
         )
 
+    lines = row_devices // 4
+    z, y, core = row // 4, lax.rem(row // 2, 2), lax.rem(row, 2)
+
+    def block(at_z, at_y, at_core):
+        return (at_z * 2 + at_y) * 2 + at_core
+
+    def hand(source, at, send_sem, recv_sem, peer):
+        return remote(source, all_ref.at[at], send_sem, recv_sem, "row", peer)
+
+    def up(step, first=False):
+        at = block(z - step, y, core)
+        source = a_ref if first else all_ref.at[at]
+        return hand(source, at, up_send.at[step], up_recv.at[step], block(z + 1, y, core))
+
+    def down(step, first=False):
+        at = block(z + step, y, core)
+        source = a_ref if first else all_ref.at[at]
+        return hand(source, at, down_send.at[step], down_recv.at[step], block(z - 1, y, core))
+
+    def over_y(at_z, first=False):
+        at = block(at_z, y, core)
+        source = a_ref if first else all_ref.at[at]
+        return hand(source, at, y_send.at[at_z], y_recv.at[at_z], block(z, 1 - y, core))
+
+    def over_core(at_z, at_y, first=False):
+        at = block(at_z, at_y, core)
+        source = a_ref if first else all_ref.at[at]
+        sem = at_z * 2 + at_y
+        return hand(source, at, core_send.at[sem], core_recv.at[sem], block(z, y, 1 - core))
+
+    def arrived(at, recv_sem, send_sem):
+        hand(all_ref.at[at], at, send_sem, recv_sem, block(z, y, 1 - core)).wait_recv()
+
+    def relay(step):
+        @pl.when(z - 1 - step >= 0)
+        def _():
+            arrived(block(z - 1 - step, y, core), up_recv.at[step], up_send.at[step])
+            if step + 1 < lines - 1:
+
+                @pl.when(z + 1 < lines)
+                def _():
+                    up(step + 1).start()
+
+            over_y(z - 1 - step).start()
+            over_core(z - 1 - step, y).start()
+
+        @pl.when(z + 1 + step < lines)
+        def _():
+            arrived(block(z + 1 + step, y, core), down_recv.at[step], down_send.at[step])
+            if step + 1 < lines - 1:
+
+                @pl.when(z >= 1)
+                def _():
+                    down(step + 1).start()
+
+            over_y(z + 1 + step).start()
+            over_core(z + 1 + step, y).start()
+
+    def cross(step):
+        at_z = lax.rem(z + step, lines)
+        arrived(block(at_z, 1 - y, core), y_recv.at[at_z], y_send.at[at_z])
+        over_core(at_z, 1 - y).start()
+
+    own_a = pltpu.make_async_copy(a_ref, all_ref.at[row], a_own)
     own_list = pltpu.make_async_copy(list_ref, lists_ref.at[row], l_own)
     for c in range(chunks):
         own_c(c).start()
     own_list.start()
+    own_a.start()
     greet(("row", "col"))
     for c in range(chunks):
         for off in range(1, col_devices):
             send_c(c, off).start()
 
+    @pl.when(z + 1 < lines)
+    def _():
+        up(0, True).start()
+
+    @pl.when(z >= 1)
+    def _():
+        down(0, True).start()
+
+    over_y(z, True).start()
+    over_core(z, y, True).start()
+
     @pl.loop(1, row_devices)
     def _(off):
         send_list(off).start()
 
+    relayed = 0
     for c in range(chunks):
+        if relayed < lines - 1:
+            relay(relayed)
+            relayed += 1
         own_c(c).wait()
         for off in range(1, col_devices):
             send_c(c, off).wait_recv()
@@ -235,7 +337,30 @@
             send_x(c, off).start()
 
         own_x(c).start()
-
+        if c == 0:
+            cross(0)
+
+    for step in range(relayed, lines - 1):
+        relay(step)
+    for step in range(1, lines):
+        cross(step)
+    own_a.wait()
+    for step in range(lines - 1):
+
+        @pl.when((z - step >= 0) & (z + 1 < lines))
+        def _():
+            up(step, step == 0).wait_send()
+
+        @pl.when((z + step < lines) & (z >= 1))
+        def _():
+            down(step, step == 0).wait_send()
+
+    for at_z in range(lines):
+        over_y(at_z).wait_send()
+        for at_y in range(2):
+            over_core(at_z, at_y).wait_send()
+            sem = at_z * 2 + at_y
+            arrived(block(at_z, at_y, 1 - core), core_recv.at[sem], core_send.at[sem])
     own_list.wait()
 
     @pl.loop(1, row_devices)
@@ -252,7 +377,7 @@
             send_x(c, off).wait()
 
 
-def spread(c_matrix, beta_values, beta_rows, alpha_list, row_devices, col_devices, chunk):
+def spread(c_matrix, beta_values, beta_rows, alpha_list, packed, row_devices, col_devices, chunk):
     rows, columns = c_matrix.shape
     pairs, _, _, width, _ = beta_values.shape
     c_tiles = jnp.moveaxis(c_matrix.reshape(rows, columns // width, width), 1, 0)
@@ -264,11 +389,13 @@
         in_specs=[
             pl.BlockSpec(memory_space=pltpu.SMEM), anywhere,
             pl.BlockSpec(memory_space=pltpu.VMEM), pl.BlockSpec(memory_space=pltpu.VMEM),
+            pl.BlockSpec(memory_space=pltpu.VMEM),
         ],
-        out_specs=[anywhere, anywhere],
+        out_specs=[anywhere, anywhere, anywhere],
         out_shape=[
             jax.ShapeDtypeStruct((chunks, row_devices, pairs, strip, chunk), jnp.bfloat16),
             jax.ShapeDtypeStruct((row_devices,) + alpha_list.shape, jnp.int32),
+            jax.ShapeDtypeStruct((row_devices,) + packed.shape, packed.dtype),
         ],
         scratch_shapes=[pltpu.VMEM((col_devices * columns // width, chunk, width), jnp.bfloat16)] * chunks
         + [pltpu.VMEM((pairs, columns, chunk), jnp.bfloat16)] * chunks
@@ -276,7 +403,11 @@
             dma((chunks,)), dma((chunks, col_devices - 1)), dma((chunks, col_devices - 1)),
             dma((chunks, row_devices - 1)), dma((chunks, row_devices - 1)), dma((chunks,)),
             dma((row_devices - 1,)), dma((row_devices - 1,)), dma,
-        ],
+        ]
+        + [dma((row_devices // 4 - 1,))] * 4
+        + [dma((row_devices // 4,))] * 2
+        + [dma((row_devices // 2,))] * 2
+        + [dma],
         compiler_params=pltpu.CompilerParams(
             collective_id=0, has_side_effects=True, vmem_limit_bytes=56 << 20
         ),
@@ -284,7 +415,7 @@
             flops=1 << 37, bytes_accessed=1 << 28, transcendentals=0
         ),
         name="spread",
-    )(beta_rows, c_tiles, beta_values, alpha_list)
+    )(beta_rows, c_tiles, beta_values, alpha_list, packed)
 
 
 def exchange_kernel(own_ref, mirror_ref, own_out, mirror_out, o_send, o_recv, m_send, m_recv, sems):
@@ -360,21 +491,22 @@
     pairs, _, _, listed, tile, _ = alpha_values.shape
     rows, chunk = groups * stretch, beta_values.shape[-1]
     c_rows = c_matrix.reshape(rows, columns)
-    alpha_all = lax.all_gather(
-        alpha_values[:, :, 0].reshape(pairs * groups, listed, tile, tile), "row"
-    )
+    alpha_tiles = alpha_values[:, :, 0].reshape(pairs * groups, listed, tile, tile)
     alpha_list = alpha_rows[:, :, 0].reshape(pairs * groups, listed)
-    own_kernels = stretch % 16 == 0 and rows % chunk == 0
+    own_kernels = stretch % 16 == 0 and rows % chunk == 0 and tile % 128 == 64
+    own_kernels = own_kernels and row_devices % 4 == 0 and pairs * groups % 2 == 0
     if own_kernels:
         entries = alpha_list.size
         padded = jnp.pad(alpha_list.reshape(-1), (0, -entries % 1024)).reshape(-1, 128)
-        x_strip, rows_all = spread(
-            c_rows, beta_values, beta_rows, padded, row_devices, col_devices, chunk
+        x_strip, rows_all, alpha_all = spread(
+            c_rows, beta_values, beta_rows, padded, pack_alpha(alpha_tiles), row_devices,
+            col_devices, chunk,
         )
         rows_all = rows_all.reshape(row_devices, -1)[:, :entries]
         rows_all = rows_all.reshape(row_devices, pairs * groups, listed)
     else:
         rows_all = lax.all_gather(alpha_list, "row")
+        alpha_all = lax.all_gather(alpha_tiles, "row")
         xt = beta_products(lax.all_gather(c_rows, "col"), beta_values, beta_rows)
         xt = jnp.moveaxis(xt.reshape(pairs, row_devices, stretch, rows), 1, 0)
         x_strip = lax.all_to_all(xt, "row", 0, 0)[None]

time: 245 us -> 194 us (0.79)
  Pallas kernels: 219 us -> 181 us
  between operations: 13.4 us -> 0.05 us
    pallas_call x1, Pallas kernels: 130 us -> 88.5 us  [spread(): pl.pallas_call(functools.partial(spread_kernel, chunks), in_specs=[pl.Blo...]
    pallas_call x1, Pallas kernels: 61.8 us -> 65.9 us  [exchange(): pl.pallas_call(exchange_kernel, in_specs=[local, local], out_specs=[anywh...]
  transfers between devices with their start and end apart: 1 -> 0, of which waited for: 1 -> 0; matrix products, arithmetic and copies ran while one was open for 4% -> 0% of each run, Pallas kernels for 53% -> 0%
where the time goes in v3:
time: 194 us; the launch traced here: 193 us
  Pallas kernels  181 us (93%)
  local copies, waits for them, and re-layouts  8.87 us (5%)
  other arithmetic  2.48 us (1%)
    pallas_call x1, Pallas kernels, spread(): pl.pallas_call(functools.partial(spread_kernel, chunks), in_specs=[pl.Blo...  88.5 us
    pallas_call x1, Pallas kernels, exchange(): pl.pallas_call(exchange_kernel, in_specs=[local, local], out_specs=[anywh...  65.9 us
    pallas_call x1, Pallas kernels, alpha_products(): pl.pallas_call(functools.partial(alpha_kernel, groups), grid_spec=pltpu.P...  18.5 us
    pallas_call x1, Pallas kernels, final(): pl.pallas_call(final_kernel, grid=(columns // block,), in_specs=[pl.Block...  8.36 us

profile of v3, /device:TPU:15, one launch (start us, length us, event | category | flops | bytes accessed | tf_op | source)
XLA Modules:
  0.0 192.7 jit_solution(12818238150262553845)
XLA Ops:
  0.0 0.0 copy-start
  0.0 0.5 broadcast.5
  0.5 1.5 reduce.3
  2.1 0.1 reshape_reshape_squeeze.6
  2.1 0.6 pad_bitcast_fusion.list_ref
  2.7 1.4 copy.11.rows_ref
  4.1 1.0 slice.16
  5.1 1.1 fusion
  6.2 0.9 maximum_maximum_fusion.a_ref
  7.1 0.0 copy-done
  7.1 0.6 copy.15
  7.7 1.9 %copy.17 = bf16[384,24,128]{2,0,1:T(8,128)(2,1)} copy(bf16[384,24,128]{2,1,0:T(8,128)(2,1)S(1)} %bitcast.15) | data formatting | bytes 4718592 | tf_op jit(solution)/shard_map/reshape;reshape | solution.py:383
  9.6 88.5 %spread.1 = (bf16[3,16,1,192,128]{4,3,2,1,0:T(8,128)(2,1)}, s32[16,8,128]{2,1,0:T(8,128)}, bf16[16,2304,128]{2,1,0:T(8,128)(2,1)}) custom-call(s32[1,24,6]{2,1,0:T(8,128)} %copy.11.rows_ref, bf16[24,384,128]{2,1,0:T(8,128)(2,1)} %bitcast.20, bf16[1,24,6,128,128]{4,3,2,1,0:T(8,128)(2,1)} %b_ref.1, s32[8,128]{1,0:T(8,128)} %pad_bitcast_fusion.list_ref, ...), custom_call_target="tpu_custom_call" | custom-call | flops 137438953472 | bytes 268435456 | tf_op jit(solution)/shard_map/spread/pallas_call | solution.py:387
  98.1 1.0 copy.14
  99.2 0.7 copy.13.rows_ref
  99.9 18.5 %alpha_products.1 = (bf16[16,192,384]{2,1,0:T(8,128)(2,1)}, bf16[2,192,3072]{2,1,0:T(8,128)(2,1)}) custom-call(s32[16,2,4]{2,1,0:T(2,128)} %copy.13.rows_ref, bf16[16,2304,128]{2,1,0:T(8,128)(2,1)} %get-tuple-element.13.a_ref, bf16[3,16,1,192,128]{4,3,2,1,0:T(8,128)(2,1)} %get-tuple-element.14.x_ref), custom_call_target="tpu_custom_call" | custom-call | tf_op jit(solution)/shard_map/alpha_products/pallas_call | solution.py:115
  118.4 65.9 %exchange.1 = (bf16[16,192,384]{2,1,0:T(8,128)(2,1)}, bf16[2,192,3072]{2,1,0:T(8,128)(2,1)}) custom-call(bf16[16,192,384]{2,1,0:T(8,128)(2,1)} %get-tuple-element.15.own_ref, bf16[2,192,3072]{2,1,0:T(8,128)(2,1)} %get-tuple-element.16.mirror_ref), custom_call_target="tpu_custom_call" | custom-call | tf_op jit(solution)/shard_map/exchange/pallas_call | solution.py:469
  184.4 8.4 %final.1 = f32[384,3072]{1,0:T(8,128)} custom-call(bf16[3072,384]{1,0:T(8,128)(2,1)} %bitcast.17, bf16[384,3072]{1,0:T(8,128)(2,1)} %bitcast.18, f32[384,3072]{1,0:T(8,128)} %bitcast.16), custom_call_target="tpu_custom_call" | custom-call | tf_op jit(solution)/shard_map/final/pallas_call | solution.py:148
  (1 shorter events, 0.0 us)
Async XLA Ops:
  0.0 7.1 %copy-start = (bf16[2,192,3072]{2,1,0:T(8,128)(2,1)S(1)}, bf16[2,192,3072]{2,1,0:T(8,128)(2,1)}, u32[]{:S(2)}) copy-start(bf16[2,192,3072]{2,1,0:T(8,128)(2,1)} %param.6) | copy-start | bytes 7077892

commit v4 on v3

--- a/solution.py
+++ b/solution.py
@@ -47,19 +47,20 @@
     )(beta_rows, gathered, beta_values)
 
 
-def pack_alpha(tiles):
-    count, listed, tile, _ = tiles.shape
-    flat = tiles.reshape(count * listed * tile, tile)
-    half, whole = flat.shape[0] // 2, tile // 128
-    parts = [flat[:, i * 128 : (i + 1) * 128] for i in range(whole)]
-    parts.append(jnp.concatenate([flat[:half, whole * 128 :], flat[half:, whole * 128 :]], axis=1))
-    return jnp.concatenate(parts, axis=0)
-
-
-def packed_product(a_ref, slot, slots, listed, tile, x):
+def pack_alpha(flat_ref, packed_ref):
+    size, tile = flat_ref.shape
+    half, whole = size // 2, tile // 128
+    for i in range(whole):
+        packed_ref[pl.ds(i * size, size), :] = flat_ref[:, i * 128 : (i + 1) * 128]
+    packed_ref[pl.ds(whole * size, half), :] = jnp.concatenate(
+        [flat_ref[pl.ds(0, half), whole * 128 :], flat_ref[pl.ds(half, half), whole * 128 :]], axis=1
+    )
+
+
+def packed_product(a_ref, at, slot, slots, listed, tile, x):
     size, whole = listed * tile, tile // 128
-    parts = [a_ref[0, pl.ds(i * slots * size + slot * size, size), :] for i in range(whole)]
-    parts.append(a_ref[0, pl.ds(whole * slots * size + slot % (slots // 2) * size, size), :])
+    parts = [a_ref[at, pl.ds(i * slots * size + slot * size, size), :] for i in range(whole)]
+    parts.append(a_ref[at, pl.ds(whole * slots * size + slot % (slots // 2) * size, size), :])
     blank = jnp.zeros((x.shape[0], 64), x.dtype)
     tail = [x[:, whole * 128 :], blank]
     if slot >= slots // 2:
@@ -80,30 +81,33 @@
     def _():
         acc_ref[...] = jnp.zeros_like(acc_ref)
 
-    for k in range(pairs):
-        parts = [x_ref[c, 0, k] for c in range(x_ref.shape[0])]
-        merged = jnp.concatenate(parts, axis=1) if len(parts) > 1 else parts[0]
-        for g in range(groups):
-            x = merged[:, g * tile : (g + 1) * tile]
-            slot = k * groups + g
-            if len(a_ref.shape) == 3:
-                product = packed_product(a_ref, slot, pairs * groups, listed, tile, x)
-                for z in range(listed):
-                    acc_ref[rows_ref[r, slot, z]] += product[z * tile : (z + 1) * tile]
-            else:
-
-                @pl.loop(0, listed)
-                def _(z):
-                    acc_ref[rows_ref[r, slot, z]] += lax.dot_general(
-                        a_ref[0, slot, z], x, CONTRACT_LAST, preferred_element_type=jnp.float32
-                    )
+    for i in range(x_ref.shape[1]):
+        at = r * x_ref.shape[1] + i
+        for k in range(pairs):
+            parts = [x_ref[c, i, k] for c in range(x_ref.shape[0])]
+            merged = jnp.concatenate(parts, axis=1) if len(parts) > 1 else parts[0]
+            for g in range(groups):
+                x = merged[:, g * tile : (g + 1) * tile]
+                slot = k * groups + g
+                if len(a_ref.shape) == 3:
+                    product = packed_product(a_ref, i, slot, pairs * groups, listed, tile, x)
+                    for z in range(listed):
+                        acc_ref[rows_ref[at, slot, z]] += product[z * tile : (z + 1) * tile]
+                else:
+
+                    @pl.loop(0, listed)
+                    def _(z):
+                        acc_ref[rows_ref[at, slot, z]] += lax.dot_general(
+                            a_ref[i, slot, z], x, CONTRACT_LAST,
+                            preferred_element_type=jnp.float32,
+                        )
 
     @pl.when(r == row_devices - 1)
     def _():
         count = acc_ref.shape[0] // groups
         for g in range(groups):
             for to in range(count):
-                turned = acc_ref[g * count + to].T.astype(own_ref.dtype)
+                turned = acc_ref[g * count + to].astype(own_ref.dtype).T
                 own_ref[to, :, g * tile : (g + 1) * tile] = turned
                 mirror_ref[g, :, to * tile : (to + 1) * tile] = turned
 
@@ -111,15 +115,16 @@
 def alpha_products(alpha_all, rows_all, x_strip, groups):
     row_devices, rest = alpha_all.shape[0], alpha_all.shape[1:]
     tile = x_strip.shape[0] * x_strip.shape[-1] // groups
+    per = 2 if len(rest) == 2 and row_devices % 2 == 0 else 1
     chunks, _, pairs, strip, chunk = x_strip.shape
     return pl.pallas_call(
         functools.partial(alpha_kernel, groups),
         grid_spec=pltpu.PrefetchScalarGridSpec(
             num_scalar_prefetch=1,
-            grid=(row_devices,),
+            grid=(row_devices // per,),
             in_specs=[
-                pl.BlockSpec((1,) + rest, lambda r, s: (r,) + (0,) * len(rest)),
-                pl.BlockSpec((chunks, 1, pairs, strip, chunk), lambda r, s: (0, r, 0, 0, 0)),
+                pl.BlockSpec((per,) + rest, lambda r, s: (r,) + (0,) * len(rest)),
+                pl.BlockSpec((chunks, per, pairs, strip, chunk), lambda r, s: (0, r, 0, 0, 0)),
             ],
             out_specs=[
                 pl.BlockSpec((row_devices, strip, groups * tile), lambda r, s: (0, 0, 0)),
@@ -137,7 +142,7 @@
 
 
 def final_kernel(own_ref, mirror_ref, gaps_ref, out_ref):
-    own = own_ref[...].astype(jnp.float32).T
+    own = own_ref[...].T.astype(jnp.float32)
     out_ref[...] = (own + mirror_ref[...].astype(jnp.float32)) / gaps_ref[...]
 
 
@@ -179,27 +184,29 @@
     )
 
 
-def spread_kernel(chunks, rows_ref, c_ref, b_ref, list_ref, a_ref, x_ref, lists_ref, all_ref, *scratch):
+def spread_kernel(chunks, rows_ref, c_ref, b_ref, list_ref, flat_ref, x_ref, lists_ref, all_ref, *scratch):
     held, sent = scratch[:chunks], scratch[chunks : 2 * chunks]
     (local_sem, c_send, c_recv, x_send, x_recv, own_sem, l_send, l_recv, l_own, up_send, up_recv,
-     down_send, down_recv, y_send, y_recv, core_send, core_recv, a_own) = scratch[2 * chunks :]
+     down_send, down_recv, y_send, y_recv, core_send, core_recv, a_own, a_ref) = scratch[2 * chunks :]
     row_devices, row = lax.axis_size("row"), lax.axis_index("row")
     col_devices, col = lax.axis_size("col"), lax.axis_index("col")
     pairs, tiles, listed, width, _ = b_ref.shape
-    per_owner, rows, _ = c_ref.shape
+    rows, columns = c_ref.shape
+    per_owner = columns // width
     chunk = rows // chunks
     strip = per_owner * width // row_devices
 
-    def own_c(c):
+    def own_c(c, t):
         return pltpu.make_async_copy(
-            c_ref.at[:, pl.ds(c * chunk, chunk)], held[c].at[pl.ds(col * per_owner, per_owner)],
-            local_sem.at[c],
-        )
-
-    def send_c(c, off):
+            c_ref.at[pl.ds(c * chunk, chunk), pl.ds(pl.multiple_of(t * width, width), width)],
+            held[c].at[col * per_owner + t], local_sem.at[c, t],
+        )
+
+    def send_c(c, off, t):
         return remote(
-            c_ref.at[:, pl.ds(c * chunk, chunk)], held[c].at[pl.ds(col * per_owner, per_owner)],
-            c_send.at[c, off - 1], c_recv.at[c, off - 1], "col", lax.rem(col + off, col_devices),
+            c_ref.at[pl.ds(c * chunk, chunk), pl.ds(pl.multiple_of(t * width, width), width)],
+            held[c].at[col * per_owner + t], c_send.at[c, off - 1, t], c_recv.at[c, off - 1, t],
+            "col", lax.rem(col + off, col_devices),
         )
 
     def send_x(c, off):
@@ -288,13 +295,20 @@
     own_a = pltpu.make_async_copy(a_ref, all_ref.at[row], a_own)
     own_list = pltpu.make_async_copy(list_ref, lists_ref.at[row], l_own)
     for c in range(chunks):
-        own_c(c).start()
+
+        @pl.loop(0, per_owner)
+        def _(t):
+            own_c(c, t).start()
+
     own_list.start()
-    own_a.start()
+    pack_alpha(flat_ref, a_ref)
     greet(("row", "col"))
     for c in range(chunks):
         for off in range(1, col_devices):
-            send_c(c, off).start()
+
+            @pl.loop(0, per_owner)
+            def _(t):
+                send_c(c, off, t).start()
 
     @pl.when(z + 1 < lines)
     def _():
@@ -306,6 +320,7 @@
 
     over_y(z, True).start()
     over_core(z, y, True).start()
+    own_a.start()
 
     @pl.loop(1, row_devices)
     def _(off):
@@ -316,9 +331,12 @@
         if relayed < lines - 1:
             relay(relayed)
             relayed += 1
-        own_c(c).wait()
-        for off in range(1, col_devices):
-            send_c(c, off).wait_recv()
+
+        @pl.loop(0, per_owner)
+        def _(t):
+            own_c(c, t).wait()
+            for off in range(1, col_devices):
+                send_c(c, off, t).wait_recv()
 
         @pl.loop(0, tiles)
         def _(j):
@@ -370,17 +388,21 @@
     for c in range(chunks):
         own_x(c).wait()
         for off in range(1, col_devices):
-            send_c(c, off).wait_send()
+
+            @pl.loop(0, per_owner)
+            def _(t):
+                send_c(c, off, t).wait_send()
 
         @pl.loop(1, row_devices)
         def _(off):
             send_x(c, off).wait()
 
 
-def spread(c_matrix, beta_values, beta_rows, alpha_list, packed, row_devices, col_devices, chunk):
+def spread(c_matrix, beta_values, beta_rows, alpha_list, flat, row_devices, col_devices, chunk):
     rows, columns = c_matrix.shape
     pairs, _, _, width, _ = beta_values.shape
-    c_tiles = jnp.moveaxis(c_matrix.reshape(rows, columns // width, width), 1, 0)
+    packed_shape = (flat.shape[0] * flat.shape[1] // 128, 128)
+    held = columns // width
     strip, chunks = columns // row_devices, rows // chunk
     dma = pltpu.SemaphoreType.DMA
     anywhere = pl.BlockSpec(memory_space=pl.ANY)
@@ -395,19 +417,20 @@
         out_shape=[
             jax.ShapeDtypeStruct((chunks, row_devices, pairs, strip, chunk), jnp.bfloat16),
             jax.ShapeDtypeStruct((row_devices,) + alpha_list.shape, jnp.int32),
-            jax.ShapeDtypeStruct((row_devices,) + packed.shape, packed.dtype),
+            jax.ShapeDtypeStruct((row_devices,) + packed_shape, flat.dtype),
         ],
         scratch_shapes=[pltpu.VMEM((col_devices * columns // width, chunk, width), jnp.bfloat16)] * chunks
         + [pltpu.VMEM((pairs, columns, chunk), jnp.bfloat16)] * chunks
         + [
-            dma((chunks,)), dma((chunks, col_devices - 1)), dma((chunks, col_devices - 1)),
+            dma((chunks, held)), dma((chunks, col_devices - 1, held)),
+            dma((chunks, col_devices - 1, held)),
             dma((chunks, row_devices - 1)), dma((chunks, row_devices - 1)), dma((chunks,)),
             dma((row_devices - 1,)), dma((row_devices - 1,)), dma,
         ]
         + [dma((row_devices // 4 - 1,))] * 4
         + [dma((row_devices // 4,))] * 2
         + [dma((row_devices // 2,))] * 2
-        + [dma],
+        + [dma, pltpu.VMEM(packed_shape, flat.dtype)],
         compiler_params=pltpu.CompilerParams(
             collective_id=0, has_side_effects=True, vmem_limit_bytes=56 << 20
         ),
@@ -415,7 +438,7 @@
             flops=1 << 37, bytes_accessed=1 << 28, transcendentals=0
         ),
         name="spread",
-    )(beta_rows, c_tiles, beta_values, alpha_list, packed)
+    )(beta_rows, c_matrix, beta_values, alpha_list, flat)
 
 
 def exchange_kernel(own_ref, mirror_ref, own_out, mirror_out, o_send, o_recv, m_send, m_recv, sems):
@@ -491,15 +514,15 @@
     pairs, _, _, listed, tile, _ = alpha_values.shape
     rows, chunk = groups * stretch, beta_values.shape[-1]
     c_rows = c_matrix.reshape(rows, columns)
-    alpha_tiles = alpha_values[:, :, 0].reshape(pairs * groups, listed, tile, tile)
-    alpha_list = alpha_rows[:, :, 0].reshape(pairs * groups, listed)
+    alpha_tiles = alpha_values.reshape(pairs * groups, listed, tile, tile)
+    alpha_list = alpha_rows.reshape(pairs * groups, listed)
     own_kernels = stretch % 16 == 0 and rows % chunk == 0 and tile % 128 == 64
     own_kernels = own_kernels and row_devices % 4 == 0 and pairs * groups % 2 == 0
     if own_kernels:
         entries = alpha_list.size
         padded = jnp.pad(alpha_list.reshape(-1), (0, -entries % 1024)).reshape(-1, 128)
         x_strip, rows_all, alpha_all = spread(
-            c_rows, beta_values, beta_rows, padded, pack_alpha(alpha_tiles), row_devices,
+            c_rows, beta_values, beta_rows, padded, alpha_tiles.reshape(-1, tile), row_devices,
             col_devices, chunk,
         )
         rows_all = rows_all.reshape(row_devices, -1)[:, :entries]

time: 194 us -> 188 us (0.969)
  local copies, waits for them, and re-layouts: 8.87 us -> 4.28 us
    pallas_call x1, Pallas kernels: 18.5 us -> 14.4 us  [alpha_products(): pl.pallas_call(functools.partial(alpha_kernel, groups), grid_spec=pltpu.P...]
    pallas_call x1, Pallas kernels: 88.5 us -> 92.4 us  [spread(): pl.pallas_call(functools.partial(spread_kernel, chunks), in_specs=[pl.Blo...]
    slice x2 -> x0, local copies, waits for them, and re-layouts: 2.07 us -> none  [the longest x1 1.05 us: pack_alpha(): flat[:half, whole * 128:]]
    another operation x1 -> x0, local copies, waits for them, and re-layouts: 1.94 us -> none  [spread(): c_matrix.reshape(rows, columns // width, width)]
where the time goes in v4:
time: 188 us; the launch traced here: 187 us
  Pallas kernels  182 us (97%)
  local copies, waits for them, and re-layouts  4.28 us (2%)
    pallas_call x1, Pallas kernels, spread(): pl.pallas_call(functools.partial(spread_kernel, chunks), in_specs=[pl.Blo...  92.4 us
    pallas_call x1, Pallas kernels, exchange(): pl.pallas_call(exchange_kernel, in_specs=[local, local], out_specs=[anywh...  66.6 us
    pallas_call x1, Pallas kernels, alpha_products(): pl.pallas_call(functools.partial(alpha_kernel, groups), grid_spec=pltpu.P...  14.4 us
    pallas_call x1, Pallas kernels, final(): pl.pallas_call(final_kernel, grid=(columns // block,), in_specs=[pl.Block...  8.27 us

profile of v4, /device:TPU:15, one launch (start us, length us, event | category | flops | bytes accessed | tf_op | source)
XLA Modules:
  0.0 187.3 jit_solution(16531588658151699601)
XLA Ops:
  0.0 0.5 broadcast.5
  0.5 1.3 reduce.3
  1.9 0.1 reshape_reshape.6
  1.9 0.6 pad_bitcast_fusion.list_ref
  2.5 1.4 copy.7.rows_ref
  3.9 92.4 %spread.1 = (bf16[3,16,1,192,128]{4,3,2,1,0:T(8,128)(2,1)}, s32[16,8,128]{2,1,0:T(8,128)}, bf16[16,2304,128]{2,1,0:T(8,128)(2,1)}) custom-call(s32[1,24,6]{2,1,0:T(8,128)} %copy.7.rows_ref, bf16[384,3072]{1,0:T(8,128)(2,1)} %bitcast.15, bf16[1,24,6,128,128]{4,3,2,1,0:T(8,128)(2,1)} %b_ref.1, s32[8,128]{1,0:T(8,128)} %pad_bitcast_fusion.list_ref, ...), custom_call_target="tpu_custom_call" | custom-call | flops 137438953472 | bytes 268435456 | tf_op jit(solution)/shard_map/spread/pallas_call | solution.py:409
  96.3 1.0 copy.10
  97.3 0.7 copy.9.rows_ref
  98.0 14.4 %alpha_products.1 = (bf16[16,192,384]{2,1,0:T(8,128)(2,1)}, bf16[2,192,3072]{2,1,0:T(8,128)(2,1)}) custom-call(s32[16,2,4]{2,1,0:T(2,128)} %copy.9.rows_ref, bf16[16,2304,128]{2,1,0:T(8,128)(2,1)} %get-tuple-element.13.a_ref, bf16[3,16,1,192,128]{4,3,2,1,0:T(8,128)(2,1)} %get-tuple-element.14.x_ref), custom_call_target="tpu_custom_call" | custom-call | tf_op jit(solution)/shard_map/alpha_products/pallas_call | solution.py:120
  112.4 66.6 %exchange.1 = (bf16[16,192,384]{2,1,0:T(8,128)(2,1)}, bf16[2,192,3072]{2,1,0:T(8,128)(2,1)}) custom-call(bf16[16,192,384]{2,1,0:T(8,128)(2,1)} %get-tuple-element.15.own_ref, bf16[2,192,3072]{2,1,0:T(8,128)(2,1)} %get-tuple-element.16.mirror_ref), custom_call_target="tpu_custom_call" | custom-call | tf_op jit(solution)/shard_map/exchange/pallas_call | solution.py:492
  179.0 8.3 %final.1 = f32[384,3072]{1,0:T(8,128)} custom-call(bf16[3072,384]{1,0:T(8,128)(2,1)} %bitcast.11, bf16[384,3072]{1,0:T(8,128)(2,1)} %bitcast.12, f32[384,3072]{1,0:T(8,128)} %bitcast.10), custom_call_target="tpu_custom_call" | custom-call | tf_op jit(solution)/shard_map/final/pallas_call | solution.py:153
  (1 shorter events, 0.0 us)

commit v5 on v4

--- a/solution.py
+++ b/solution.py
@@ -115,7 +115,7 @@
 def alpha_products(alpha_all, rows_all, x_strip, groups):
     row_devices, rest = alpha_all.shape[0], alpha_all.shape[1:]
     tile = x_strip.shape[0] * x_strip.shape[-1] // groups
-    per = 2 if len(rest) == 2 and row_devices % 2 == 0 else 1
+    per = 4 if len(rest) == 2 and row_devices % 4 == 0 else 1
     chunks, _, pairs, strip, chunk = x_strip.shape
     return pl.pallas_call(
         functools.partial(alpha_kernel, groups),
@@ -177,6 +177,11 @@
     pl.semaphore_wait(barrier, total)
 
 
+def alternate(step, size):
+    odd = lax.rem(step, 2)
+    return odd * ((step + 1) // 2) + (1 - odd) * (size - step // 2)
+
+
 def remote(src, dst, send_sem, recv_sem, axis, peer):
     return pltpu.make_async_remote_copy(
         src_ref=src, dst_ref=dst, send_sem=send_sem, recv_sem=recv_sem,
@@ -352,7 +357,7 @@
 
         @pl.loop(1, row_devices)
         def _(off):
-            send_x(c, off).start()
+            send_x(c, alternate(off, row_devices)).start()
 
         own_x(c).start()
         if c == 0:
@@ -468,7 +473,7 @@
 
     @pl.loop(1, row_devices)
     def _(off):
-        send_own(off).start()
+        send_own(alternate(off, row_devices)).start()
 
     stay_own.start()
     stay_mirror.start()

time: 188 us -> 185 us (0.984)
  the two profiles are of different devices: /device:TPU:15 before, /device:TPU:0 now
where the time goes in v5:
time: 185 us; the launch traced here: 184 us
  Pallas kernels  179 us (97%)
  local copies, waits for them, and re-layouts  4.28 us (2%)
    pallas_call x1, Pallas kernels, spread(): pl.pallas_call(functools.partial(spread_kernel, chunks), in_specs=[pl.Blo...  98.6 us
    pallas_call x1, Pallas kernels, exchange(): pl.pallas_call(exchange_kernel, in_specs=[local, local], out_specs=[anywh...  59.2 us
    pallas_call x1, Pallas kernels, alpha_products(): pl.pallas_call(functools.partial(alpha_kernel, groups), grid_spec=pltpu.P...  12.5 us
    pallas_call x1, Pallas kernels, final(): pl.pallas_call(final_kernel, grid=(columns // block,), in_specs=[pl.Block...  8.27 us

profile of v5, /device:TPU:0, one launch (start us, length us, event | category | flops | bytes accessed | tf_op | source)
XLA Modules:
  0.0 184.2 jit_solution(16022220115843045673)
XLA Ops:
  0.0 0.5 broadcast.5
  0.5 1.3 reduce.3
  1.9 0.1 reshape_reshape.6
  1.9 0.6 pad_bitcast_fusion.list_ref
  2.5 1.4 copy.7.rows_ref
  3.9 98.6 %spread.1 = (bf16[3,16,1,192,128]{4,3,2,1,0:T(8,128)(2,1)}, s32[16,8,128]{2,1,0:T(8,128)}, bf16[16,2304,128]{2,1,0:T(8,128)(2,1)}) custom-call(s32[1,24,6]{2,1,0:T(8,128)} %copy.7.rows_ref, bf16[384,3072]{1,0:T(8,128)(2,1)} %bitcast.15, bf16[1,24,6,128,128]{4,3,2,1,0:T(8,128)(2,1)} %b_ref.1, s32[8,128]{1,0:T(8,128)} %pad_bitcast_fusion.list_ref, ...), custom_call_target="tpu_custom_call" | custom-call | flops 137438953472 | bytes 268435456 | tf_op jit(solution)/shard_map/spread/pallas_call | solution.py:414
  102.5 1.0 copy.10
  103.5 0.7 copy.9.rows_ref
  104.2 12.5 %alpha_products.1 = (bf16[16,192,384]{2,1,0:T(8,128)(2,1)}, bf16[2,192,3072]{2,1,0:T(8,128)(2,1)}) custom-call(s32[16,2,4]{2,1,0:T(2,128)} %copy.9.rows_ref, bf16[16,2304,128]{2,1,0:T(8,128)(2,1)} %get-tuple-element.13.a_ref, bf16[3,16,1,192,128]{4,3,2,1,0:T(8,128)(2,1)} %get-tuple-element.14.x_ref), custom_call_target="tpu_custom_call" | custom-call | tf_op jit(solution)/shard_map/alpha_products/pallas_call | solution.py:120
  116.7 59.2 %exchange.1 = (bf16[16,192,384]{2,1,0:T(8,128)(2,1)}, bf16[2,192,3072]{2,1,0:T(8,128)(2,1)}) custom-call(bf16[16,192,384]{2,1,0:T(8,128)(2,1)} %get-tuple-element.15.own_ref, bf16[2,192,3072]{2,1,0:T(8,128)(2,1)} %get-tuple-element.16.mirror_ref), custom_call_target="tpu_custom_call" | custom-call | tf_op jit(solution)/shard_map/exchange/pallas_call | solution.py:497
  175.9 8.3 %final.1 = f32[384,3072]{1,0:T(8,128)} custom-call(bf16[3072,384]{1,0:T(8,128)(2,1)} %bitcast.11, bf16[384,3072]{1,0:T(8,128)(2,1)} %bitcast.12, f32[384,3072]{1,0:T(8,128)} %bitcast.10), custom_call_target="tpu_custom_call" | custom-call | tf_op jit(solution)/shard_map/final/pallas_call | solution.py:153
  (1 shorter events, 0.0 us)
